TPU v7x, 32 devices: a whole 2x2x4 slice. The times are simulated.
32 devices in a mesh: fsdp: 8 (over y, x, core), tp: 4 (over z).
Axes of the slice: x: 2, y: 2, z: 4, core: 2. Of those that a mesh axis runs over, the one named last changes fastest.
Arguments:
- layer_input: bfloat16 [8192, 2048], P(('fsdp', 'tp')), may hold values from -6 to 6
- teacher: bfloat16 [8192, 2048], P(('fsdp', 'tp')), may hold values from -6 to 6
- out_grad: bfloat16 [8192, 2048], P(('fsdp', 'tp')), may hold values from -6 to 6
- lengths: int32 [8], P('fsdp'), may hold values from 512 to 1024, as said below
- norm_gain: float32 [2048], P(('fsdp', 'tp')), may hold values from 0.5 to 1.5
- norm_bias: float32 [2048], P(('fsdp', 'tp')), may hold values from -4 to 4
- qkv_weight: bfloat16 [3, 2048, 2048], P(None, 'fsdp', 'tp'), may hold values from -0.125 to 0.125
- qkv_bias: bfloat16 [3, 2048], P(None, ('tp', 'fsdp')), may hold values from -4 to 4
- out_weight: bfloat16 [2048, 2048], P('tp', 'fsdp'), may hold values from -1 to 1
- gate_up_weight: bfloat16 [2, 2048, 5632], P(None, 'fsdp', 'tp'), may hold values from -0.125 to 0.125
- down_weight: bfloat16 [5632, 2048], P('tp', 'fsdp'), may hold values from -0.078125 to 0.078125
Outputs:
- output: bfloat16 [8192, 2048], P(('fsdp', 'tp'))
- loss: float32 [], replicated
- input_grad: bfloat16 [8192, 2048], P(('fsdp', 'tp'))
- norm_gain_grad: float32 [2048], P(('fsdp', 'tp'))
- norm_bias_grad: float32 [2048], P(('fsdp', 'tp'))
- qkv_weight_grad: float32 [3, 2048, 2048], P(None, 'fsdp', 'tp')
- qkv_bias_grad: float32 [3, 2048], P(None, ('tp', 'fsdp'))
- out_weight_grad: float32 [2048, 2048], P('tp', 'fsdp')
- gate_up_weight_grad: float32 [2, 2048, 5632], P(None, 'fsdp', 'tp')
- down_weight_grad: float32 [5632, 2048], P('tp', 'fsdp')
Inputs may be any that keep to these rules, and one draw needn't show every extreme that they name: `lengths`: each slot holds at least half of its 1024 positions; some slot is full in every draw.
All inputs are finite; a program needn't handle non-finite values.
Results may differ from a plain program's by a relative error of at most 0.0084.
Values may be sent and summed in bfloat16 or wider, within the bound.
No kernel may reach another device: no remote copies, remote signals or barrier semaphores. Data moves between devices by JAX's collectives and lax.ppermute only.
A program may use at most 256 MiB of HBM per device.

v0:
```python
import jax
import jax.numpy as jnp
from jax import lax
from jax.sharding import PartitionSpec as P

D = 2048
HD = 64
ROT = 16
SEQ = 1024
SEQS_DEV = 1
epsilon = 1e-05


def rotary_tables(row_total):
    half_rot = ROT // 2
    positions = (jnp.arange(row_total, dtype=jnp.int32) % SEQ).astype(jnp.float32)
    frequency = 10000.0 ** (-2.0 * jnp.arange(half_rot, dtype=jnp.float32) / ROT)
    angles = positions[:, None] * frequency[None, :]
    angles = jnp.concatenate([angles, angles], -1)[:, None, :]
    return (jnp.cos(angles), jnp.sin(angles))


def turn_heads(vectors, cos_tab, sine_tab):
    half_rot = ROT // 2
    head_part = vectors[..., :ROT]
    turned = jnp.concatenate([-head_part[..., half_rot:], head_part[..., :half_rot]], -1)
    return jnp.concatenate([head_part * cos_tab + turned * sine_tab, vectors[..., ROT:]], -1)


def unturn_heads(vectors, cos_tab, sine_tab):
    half_rot = ROT // 2
    head_part = vectors[..., :ROT]
    by_sine = head_part * sine_tab
    back_part = jnp.concatenate([by_sine[..., half_rot:], -by_sine[..., :half_rot]], -1)
    return jnp.concatenate([head_part * cos_tab + back_part, vectors[..., ROT:]], -1)


def per_device(
    layer_input,
    teacher,
    out_grad,
    lengths,
    norm_gain,
    norm_bias,
    qkv_weight,
    qkv_bias,
    out_weight,
    gate_up_weight,
    down_weight,
):
    local_rows = layer_input.shape[0]
    group_rows = SEQS_DEV * SEQ
    gain_vec, shift_vec = (
        lax.all_gather(norm_gain, ("fsdp", "tp"), axis=0, tiled=True),
        lax.all_gather(norm_bias, ("fsdp", "tp"), axis=0, tiled=True),
    )
    w_qkv, b_qkv, w_out, w_gu, w_down = (
        lax.all_gather(qkv_weight, "fsdp", axis=1, tiled=True),
        lax.all_gather(qkv_bias, "fsdp", axis=1, tiled=True),
        lax.all_gather(out_weight, "fsdp", axis=1, tiled=True),
        lax.all_gather(gate_up_weight, "fsdp", axis=1, tiled=True),
        lax.all_gather(down_weight, "fsdp", axis=1, tiled=True),
    )
    row_ids = lax.axis_index("tp") * local_rows + jnp.arange(local_rows, dtype=jnp.int32)
    row_pick = (row_ids // SEQ)[:, None] == jnp.arange(SEQS_DEV, dtype=jnp.int32)[None, :]
    row_length = jnp.sum(jnp.where(row_pick, lengths[None, :], 0), 1)
    valid_rows = (row_ids % SEQ < row_length).astype(jnp.float32)
    inputs = layer_input.astype(jnp.float32)
    center = inputs - jnp.mean(inputs, -1, keepdims=True)
    inv_std = lax.rsqrt(jnp.mean(center * center, -1, keepdims=True) + epsilon)
    unit_rows = center * inv_std
    normed = (unit_rows * gain_vec + shift_vec).astype(jnp.bfloat16)
    all_normed = lax.all_gather(normed, "tp", axis=0, tiled=True)
    local_width = w_qkv.shape[2]
    local_heads = local_width // HD
    cos_tab, sine_tab = rotary_tables(group_rows)
    joined_qkv = jnp.einsum(
        "sd,jde->jse", all_normed, w_qkv, preferred_element_type=jnp.float32
    ) + b_qkv[:, None, :].astype(jnp.float32)
    queries = turn_heads(
        joined_qkv[0].reshape(group_rows, local_heads, HD), cos_tab, sine_tab
    ).astype(jnp.bfloat16)
    key_rows = turn_heads(
        joined_qkv[1].reshape(group_rows, local_heads, HD), cos_tab, sine_tab
    ).astype(jnp.bfloat16)
    values = joined_qkv[2].reshape(group_rows, local_heads, HD).astype(jnp.bfloat16)
    span_rows = min(512, SEQ)
    score_scale = HD ** (-0.5)
    key_pos = jnp.arange(SEQ, dtype=jnp.int32)
    block_count = group_rows // span_rows
    block_ids = jnp.arange(block_count, dtype=jnp.int32)

    def block_scores(block_id):
        row_start = block_id * span_rows
        seq_start = row_start // SEQ * SEQ
        q_block = lax.dynamic_slice_in_dim(queries, row_start, span_rows, 0)
        scores = (
            jnp.einsum("qhe,khe->hqk", q_block, key_rows, preferred_element_type=jnp.float32)
            * score_scale
        )
        query_pos = row_start - seq_start + jnp.arange(span_rows, dtype=jnp.int32)
        allowed = (key_pos[None, :] <= query_pos[:, None])[None]
        scores = jnp.where(allowed, scores, -1e30)
        return (row_start, seq_start, q_block, key_rows, values, scores, allowed)

    def attend(block_id):
        row_start, seq_start, q_block, k_seq, v_seq, scores, allowed = block_scores(block_id)
        row_max = jnp.max(scores, -1, keepdims=True)
        shifted = jnp.exp(scores - row_max)
        totals = jnp.sum(shifted, -1, keepdims=True)
        weights = (shifted / totals).astype(jnp.bfloat16)
        out_block = jnp.einsum("hqk,khe->qhe", weights, v_seq, preferred_element_type=jnp.float32)
        return (out_block, row_max + jnp.log(totals))

    attended, log_sums = lax.map(attend, block_ids)
    attn_rows = attended.reshape(group_rows, local_width).astype(jnp.bfloat16)
    gate_up = jnp.einsum("sd,jdf->jsf", all_normed, w_gu, preferred_element_type=jnp.float32)
    sigmoid_gate = jax.nn.sigmoid(gate_up[0])
    hidden = (gate_up[0] * sigmoid_gate * gate_up[1]).astype(jnp.bfloat16)
    branch_sum = lax.psum_scatter(
        jnp.dot(attn_rows, w_out, preferred_element_type=jnp.float32)
        + jnp.dot(hidden, w_down, preferred_element_type=jnp.float32),
        "tp",
        scatter_dimension=0,
        tiled=True,
    )
    result = inputs + valid_rows[:, None] * branch_sum
    mismatch = result - teacher.astype(jnp.float32)
    loss_part = jnp.sum(valid_rows[:, None] * mismatch * mismatch)
    count_part = jnp.sum(valid_rows)
    loss_total, valid_total = lax.psum((loss_part, count_part), ("fsdp", "tp"))
    loss_value = loss_total / (valid_total * D)
    seed_rows = valid_rows[:, None] * (out_grad.astype(jnp.float32) + mismatch)
    all_seed = lax.all_gather(seed_rows.astype(jnp.bfloat16), "tp", axis=0, tiled=True)
    w_qkv, w_out, w_gu, w_down = (
        lax.all_gather(qkv_weight, "fsdp", axis=1, tiled=True),
        lax.all_gather(out_weight, "fsdp", axis=1, tiled=True),
        lax.all_gather(gate_up_weight, "fsdp", axis=1, tiled=True),
        lax.all_gather(down_weight, "fsdp", axis=1, tiled=True),
    )
    grad_out_w = jnp.einsum("sa,sd->ad", attn_rows, all_seed, preferred_element_type=jnp.float32)
    grad_attn = (
        jnp.einsum("sd,ad->sa", all_seed, w_out, preferred_element_type=jnp.float32)
        .astype(jnp.bfloat16)
        .reshape(group_rows, local_heads, HD)
    )
    grad_down = jnp.einsum("sf,sd->fd", hidden, all_seed, preferred_element_type=jnp.float32)
    grad_hidden = jnp.einsum("sd,fd->sf", all_seed, w_down, preferred_element_type=jnp.float32)
    grad_gate = grad_hidden * gate_up[1] * sigmoid_gate * (1.0 + gate_up[0] * (1.0 - sigmoid_gate))
    grad_up = grad_hidden * gate_up[0] * sigmoid_gate
    grad_gu = jnp.stack([grad_gate, grad_up]).astype(jnp.bfloat16)
    grad_gu_w = jnp.einsum("sd,jsf->jdf", all_normed, grad_gu, preferred_element_type=jnp.float32)

    def attend_back(kv_grads, block_id):
        grad_keys, grad_values = kv_grads
        row_start, seq_start, q_block, k_seq, v_seq, scores, allowed = block_scores(block_id)
        probs = jnp.where(allowed, jnp.exp(scores - log_sums[block_id]), 0.0)
        d_block = lax.dynamic_slice_in_dim(grad_attn, row_start, span_rows, 0)
        grad_probs = jnp.einsum("qhe,khe->hqk", d_block, v_seq, preferred_element_type=jnp.float32)
        inner = jnp.sum(probs * grad_probs, -1, keepdims=True)
        grad_scores = (probs * (grad_probs - inner)).astype(jnp.bfloat16)
        grad_query = (
            jnp.einsum("hqk,khe->qhe", grad_scores, k_seq, preferred_element_type=jnp.float32)
            * score_scale
        )
        key_part = (
            jnp.einsum("hqk,qhe->khe", grad_scores, q_block, preferred_element_type=jnp.float32)
            * score_scale
        )
        value_part = jnp.einsum(
            "hqk,qhe->khe", probs.astype(jnp.bfloat16), d_block, preferred_element_type=jnp.float32
        )
        key_now = grad_keys
        grad_keys = key_now + key_part
        value_now = grad_values
        grad_values = value_now + value_part
        return ((grad_keys, grad_values), grad_query)

    zero_heads = jnp.zeros((group_rows, local_heads, HD), jnp.float32)
    (grad_keys, grad_values), grad_queries = lax.scan(
        attend_back, (zero_heads, zero_heads), block_ids
    )
    grad_queries = grad_queries.reshape(group_rows, local_heads, HD)
    grad_qkv = (
        jnp.stack(
            [
                unturn_heads(grad_queries, cos_tab, sine_tab),
                unturn_heads(grad_keys, cos_tab, sine_tab),
                grad_values,
            ]
        )
        .reshape(3, group_rows, local_width)
        .astype(jnp.bfloat16)
    )
    grad_bias = jnp.sum(grad_qkv, 1, dtype=jnp.float32)
    grad_qkv_w = jnp.einsum("sd,jse->jde", all_normed, grad_qkv, preferred_element_type=jnp.float32)
    grad_normed = lax.psum_scatter(
        jnp.einsum("jse,jde->sd", grad_qkv, w_qkv, preferred_element_type=jnp.float32)
        + jnp.einsum("jsf,jdf->sd", grad_gu, w_gu, preferred_element_type=jnp.float32),
        "tp",
        scatter_dimension=0,
        tiled=True,
    )
    gain_grad_part = jnp.sum(grad_normed * unit_rows, 0)
    bias_grad_part = jnp.sum(grad_normed, 0)
    grad_unit = grad_normed * gain_vec
    grad_inputs = inv_std * (
        grad_unit
        - jnp.mean(grad_unit, -1, keepdims=True)
        - unit_rows * jnp.mean(grad_unit * unit_rows, -1, keepdims=True)
    )
    input_grad = (seed_rows + grad_inputs).astype(jnp.bfloat16)
    gain_grad, bias_grad = (
        lax.psum_scatter(gain_grad_part, ("fsdp", "tp"), scatter_dimension=0, tiled=True),
        lax.psum_scatter(bias_grad_part, ("fsdp", "tp"), scatter_dimension=0, tiled=True),
    )
    qkv_w_grad, qkv_b_grad, out_w_grad, gu_w_grad, down_w_grad = (
        lax.psum_scatter(grad_qkv_w, "fsdp", scatter_dimension=1, tiled=True),
        lax.psum_scatter(grad_bias, "fsdp", scatter_dimension=1, tiled=True),
        lax.psum_scatter(grad_out_w, "fsdp", scatter_dimension=1, tiled=True),
        lax.psum_scatter(grad_gu_w, "fsdp", scatter_dimension=1, tiled=True),
        lax.psum_scatter(grad_down, "fsdp", scatter_dimension=1, tiled=True),
    )
    return (
        result.astype(jnp.bfloat16),
        loss_value,
        input_grad,
        gain_grad,
        bias_grad,
        qkv_w_grad,
        qkv_b_grad,
        out_w_grad,
        gu_w_grad,
        down_w_grad,
    )


def solution(mesh):
    placed = (
        P(("fsdp", "tp"), None),
        P(("fsdp", "tp"), None),
        P(("fsdp", "tp"), None),
        P("fsdp"),
        P(("fsdp", "tp")),
        P(("fsdp", "tp")),
        P(None, "fsdp", "tp"),
        P(None, ("tp", "fsdp")),
        P("tp", "fsdp"),
        P(None, "fsdp", "tp"),
        P("tp", "fsdp"),
    )
    return jax.shard_map(
        per_device,
        mesh=mesh,
        in_specs=placed,
        out_specs=(
            P(("fsdp", "tp"), None),
            P(),
            P(("fsdp", "tp"), None),
            P(("fsdp", "tp")),
            P(("fsdp", "tp")),
            P(None, "fsdp", "tp"),
            P(None, ("tp", "fsdp")),
            P("tp", "fsdp"),
            P(None, "fsdp", "tp"),
            P("tp", "fsdp"),
        ),
        check_vma=False,
    )
```

profile of v0, /device:TPU:0, one launch (start us, length us, event | category | flops | bytes accessed | tf_op | source)
XLA Modules:
  0.0 1318.2 jit_solution(7497582739152333700)
XLA Ops:
  12.2 42.0 %all-reduce.5 = (f32[2048]{0:T(1024)S(1)}, f32[2048]{0:T(1024)S(1)}) all-reduce(f32[2048]{0:T(1024)S(1)} %dynamic-update-slice.1, f32[2048]{0:T(1024)S(1)} %dynamic-update-slice), channel_id=1, replica_groups=mesh['fsdp'=8,'tp'=4] {'fsdp','tp'}, use_global_device_ids=true, to_apply=%add.1 | all-reduce | flops 4096 | bytes 32768
  60.2 10.2 all-gather
  70.7 67.1 %all-gather.8.cloned.1.call-done = bf16[1024,2048]{1,0:T(8,128)(2,1)} async-done(((bf16[256,2048]{1,0:T(8,128)(2,1)}), bf16[1024,2048]{1,0:T(8,128)(2,1)}) %all-gather.8.cloned.1.call-update) | async-done | bytes 4194320 | tf_op jit(solution)/shard_map/all_gather | solution.py:73
  137.8 47.7 %all-gather.10.cloned.1.call-done = bf16[3,2048,512]{1,2,0:T(8,128)(2,1)} async-done(((bf16[3,256,512]{1,2,0:T(8,128)(2,1)}), bf16[3,2048,512]{1,2,0:T(8,128)(2,1)}) %all-gather.10.cloned.1.call-update) | async-done | bytes 6291472 | tf_op jit(solution)/shard_map/all_gather | solution.py:58
  185.4 10.1 add_bitcast_fusion
  199.0 32.1 %while.32 = (s32[]{:T(128)}, bf16[2,512,8,64]{1,3,2,0:T(8,128)(2,1)S(1)}, f32[2,8,512,1]{2,1,3,0:T(8,128)S(1)}, s32[2]{0:T(128)S(1)}, bf16[1024,8,64]{0,2,1:T(8,...) while((s32[]{:T(128)}, ...), condition=%wide.region_5.6_spmd.clone, body=%wide.region_2.5_spmd.clone.sunk | while | flops 1124594176 | bytes 56234364 | solution.py:115
  232.5 22.6 %all-gather.14.cloned.1.call-done = bf16[2,2048,1408]{2,1,0:T(8,128)(2,1)} async-done(((bf16[2,256,1408]{2,1,0:T(8,128)(2,1)}), bf16[2,2048,1408]{2,1,0:T(8,128)(2,1)}) %all-gather.14.cloned.1.call-update) | async-done | bytes 11534352 | tf_op jit(solution)/shard_map/all_gather | solution.py:61
  255.1 17.2 %convolution_bitcast_fusion.1 = f32[2,1024,1408]{2,1,0:T(8,128)S(1)} fusion(bf16[2,2048,1408]{2,1,0:T(8,128)(2,1)} %all-gather.14.cloned.1.call-done, bf16[1024,2048]{1,0:T(8,128)(2,1)} %all-gather.8.cloned.1.call-done), kind=kOutput, calls=%fused_computation.41 | convolution fusion | flops 11811160064 | bytes 27262976 | tf_op jit(solution)/shard_map/sd,jdf->jsf/dot_general | solution.py:117
  279.3 21.9 %all-gather.16.cloned.1.call-done = bf16[1408,2048]{1,0:T(8,128)(2,1)} async-done(((bf16[1408,256]{1,0:T(8,128)(2,1)}), bf16[1408,2048]{1,0:T(8,128)(2,1)}) %all-gather.16.cloned.1.call-update) | async-done | bytes 5767184 | tf_op jit(solution)/shard_map/all_gather | solution.py:62
  301.2 11.6 fusion.74
  312.8 18.3 %all-gather.12.cloned.1.call-done = bf16[512,2048]{1,0:T(8,128)(2,1)} async-done(((bf16[512,256]{1,0:T(8,128)(2,1)}), bf16[512,2048]{1,0:T(8,128)(2,1)}) %all-gather.12.cloned.1.call-update) | async-done | bytes 2097168 | tf_op jit(solution)/shard_map/all_gather | solution.py:60
  331.2 9.7 convolution_add_fusion
  341.7 143.8 %reduce-scatter.10.cloned.1.call-done = f32[256,2048]{1,0:T(8,128)} async-done(((f32[1024,2048]{1,0:T(8,128)}), f32[256,2048]{1,0:T(8,128)}) %reduce-scatter.10.cloned.1.call-update) | async-done | bytes 2097168 | tf_op jit(solution)/shard_map/reduce_scatter | solution.py:120
  489.3 81.6 %all-gather.18.cloned.1.call-done = bf16[1024,2048]{1,0:T(8,128)(2,1)} async-done(((bf16[256,2048]{1,0:T(8,128)(2,1)}), bf16[1024,2048]{1,0:T(8,128)(2,1)}) %all-gather.18.cloned.1.call-update) | async-done | bytes 4194320 | tf_op jit(solution)/shard_map/all_gather | solution.py:134
  577.1 134.3 %while.33 = (s32[]{:T(128)}, f32[1024,8,64]{0,2,1:T(8,128)}, f32[1024,8,64]{0,2,1:T(8,128)}, f32[2,512,8,64]{1,0,3,2:T(2,128)}, s32[2]{0:T(128)S(1)}, /*index=5*...) while((s32[]{:T(128)}, f32[1024,8,64]{0,2,1:T(8,128)}, ...), condition=%wide.region_13.14_spmd.clone, body=%wide.region_11.13_spmd.clone.sunk | while | flops 2729701888 | bytes 200626816 | solution.py:180
  586.2 12.2 multiply_reduce_fusion.3
  624.3 19.7 %dynamic_update_slice.30 = f32[2,512,8,64]{1,0,3,2:T(2,128)} dynamic-update-slice(f32[2,512,8,64]{1,0,3,2:T(2,128)} %get-tuple-element.597, f32[1,512,8,64]{1,0,3,2:T(1,128)} %copy.85, s32[]{:T(128)S(6)} %copy.104, s32[]{:T(128)} %constant.200.clone.1..sunk.1, s32[]{:T(128)} %constant.200.clone.1..sunk.1, s32[]{:T(128)} %constant.200.clone.1..sunk.1) | dynamic-update-slice | bytes 2097156 | tf_op jit(solution)/shard_map/while/body/jit(dynamic_update_index_in_dim)/dynamic_update_slice | solution.py:115
  652.8 12.3 multiply_reduce_fusion.3
  674.4 9.5 bitcast_add_fusion.6
  691.6 19.7 %dynamic_update_slice.30 = f32[2,512,8,64]{1,0,3,2:T(2,128)} dynamic-update-slice(f32[2,512,8,64]{1,0,3,2:T(2,128)} %get-tuple-element.597, f32[1,512,8,64]{1,0,3,2:T(1,128)} %copy.85, s32[]{:T(128)S(6)} %copy.104, s32[]{:T(128)} %constant.200.clone.1..sunk.1, s32[]{:T(128)} %constant.200.clone.1..sunk.1, s32[]{:T(128)} %constant.200.clone.1..sunk.1) | dynamic-update-slice | bytes 2097156 | tf_op jit(solution)/shard_map/while/body/jit(dynamic_update_index_in_dim)/dynamic_update_slice | solution.py:115
  726.8 15.7 %fusion.34 = (bf16[1,1024,1408]{2,1,0:T(8,128)(2,1)}, bf16[1,1024,1408]{2,1,0:T(8,128)(2,1)}) fusion(f32[2,1024,1408]{2,1,0:T(8,128)} %copy-done.8, bf16[1024,2048]{1,0:T(8,128)(2,1)} %all-gather.18.cloned.1.call-done, bf16[1408,2048]{1,0:T(8,128)(2,1)} %all-gather.16.cloned.1.call-done), kind=kOutput, calls=%fused_computation.64 | convolution fusion | flops 5924323328 | bytes 27262976 | tf_op jit(solution)/shard_map/sd,fd->sf/dot_general | solution.py:148
  742.5 10.8 fusion.69
  753.3 20.0 %bitcast_add_fusion.2 = f32[1024,2048]{1,0:T(8,128)} fusion(f32[1024,2048,1]{1,0,2:T(8,128)} %fusion.69, bf16[2,2048,1408]{2,1,0:T(8,128)(2,1)} %all-gather.14.cloned.1.call-done, bf16[1,1024,1408]{2,1,0:T(8,128)(2,1)} %get-tuple-element.399, bf16[1,1024,1408]{2,1,0:T(8,128)(2,1)} %get-tuple-element.398), kind=kOutput, calls=%fused_computation.40 | convolution fusion | flops 11816140800 | bytes 34078720 | tf_op jit(solution)/shard_map/jsf,jdf->sd/dot_general | solution.py:199
  773.3 12.2 convolution_bitcast_fusion.2
  787.4 19.1 %convolution_bitcast_fusion = f32[2,2048,1408]{1,2,0:T(8,128)} fusion(bf16[1024,2048]{1,0:T(8,128)(2,1)} %all-gather.8.cloned.1.call-done, bf16[1,1024,1408]{2,1,0:T(8,128)(2,1)} %get-tuple-element.399, bf16[1,1024,1408]{2,1,0:T(8,128)(2,1)S(1)} %copy-done.30), kind=kOutput, calls=%fused_computation.39 | convolution fusion | flops 11814043648 | bytes 33030144 | tf_op jit(solution)/shard_map/sd,jsf->jdf/dot_general | solution.py:152
  816.1 10.8 fusion.76
  829.3 87.1 %reduce-scatter.12.cloned.1.call-done = f32[256,2048]{1,0:T(8,128)} async-done(((f32[1024,2048]{1,0:T(8,128)}), f32[256,2048]{1,0:T(8,128)}) %reduce-scatter.12.cloned.1.call-update) | async-done | bytes 2097168 | tf_op jit(solution)/shard_map/reduce_scatter | solution.py:197
  920.6 41.6 %all-reduce.4 = (f32[]{:T(128)}, f32[]{:T(128)}, f32[2048]{0:T(1024)S(1)}, f32[2048]{0:T(1024)S(1)}) all-reduce(f32[]{:T(128)} %get-tuple-element.353, f32[]{:T(128)} %fusion.68, f32[2048]{0:T(1024)S(1)} %get-tuple-element.349, f32[2048]{0:T(1024)S(1)} %get-tuple-element.352), channel_id=1, replica_groups=mesh['fsdp'=8,'tp'=4] {'fsdp','tp'}, use_global_device_ids=true, to_apply=%region_8.9 | all-reduce | flops 4098 | bytes 32784 | tf_op jit(solution)/shard_map/psum | solution.py:131
  969.7 44.2 %reduce-scatter.14.cloned.1.call-done = f32[3,256,512]{1,2,0:T(8,128)} async-done(((f32[3,2048,512]{1,2,0:T(8,128)}), f32[3,256,512]{1,2,0:T(8,128)}) %reduce-scatter.14.cloned.1.call-update) | async-done | bytes 1572880 | tf_op jit(solution)/shard_map/reduce_scatter | solution.py:218
  1016.9 147.0 %reduce-scatter.18.cloned.1.call-done = f32[2,256,1408]{1,2,0:T(8,128)} async-done(((f32[2,2048,1408]{1,2,0:T(8,128)}), f32[2,256,1408]{1,2,0:T(8,128)}) %reduce-scatter.18.cloned.1.call-update) | async-done | bytes 2883600 | tf_op jit(solution)/shard_map/reduce_scatter | solution.py:221
  1167.3 52.1 %reduce-scatter.16.cloned.1.call-done = f32[512,256]{1,0:T(8,128)} async-done(((f32[512,2048]{1,0:T(8,128)}), f32[512,256]{1,0:T(8,128)}) %reduce-scatter.16.cloned.1.call-update) | async-done | bytes 524304 | tf_op jit(solution)/shard_map/reduce_scatter | solution.py:220
  1219.4 90.9 %reduce-scatter.20.cloned.1.call-done = f32[1408,256]{1,0:T(8,128)} async-done(((f32[1408,2048]{1,0:T(8,128)}), f32[1408,256]{1,0:T(8,128)}) %reduce-scatter.20.cloned.1.call-update) | async-done | bytes 1441808 | tf_op jit(solution)/shard_map/reduce_scatter | solution.py:222
  (197 shorter events, 164.1 us)
Async XLA Ops:
  7.2 49.8 %copy-start.14 = (bf16[3,256,512]{2,1,0:T(8,128)(2,1)S(1)}, bf16[3,256,512]{2,1,0:T(8,128)(2,1)}, u32[]{:S(2)}) copy-start(bf16[3,256,512]{2,1,0:T(8,128)(2,1)} %param.21) | copy-start | bytes 2359300
  7.2 130.6 %all-gather.8.cloned.1.call-start = ((), (), s32[]{:S(2)}) async-start(), calls=%async_computation.7 | async-start | bytes 5242880 | tf_op jit(solution)/shard_map/all_gather | solution.py:73
  8.8 49.4 %copy-start.23 = (f32[256]{0:T(256)}, f32[256]{0:T(256)S(1)}, u32[]{:S(2)}) copy-start(f32[256]{0:T(256)S(1)} %broadcast_multiply_fusion.3) | copy-start | bytes 3076
  10.4 48.5 %copy-start.25 = (f32[256]{0:T(256)}, f32[256]{0:T(256)S(1)}, u32[]{:S(2)}) copy-start(f32[256]{0:T(256)S(1)} %add_rsqrt_fusion) | copy-start | bytes 3076
  56.9 128.6 %all-gather.10.cloned.1.call-start = ((), (), s32[]{:S(2)}) async-start(), calls=%async_computation.8 | async-start | bytes 7077888 | tf_op jit(solution)/shard_map/all_gather | solution.py:58
  58.1 196.9 %all-gather.14.cloned.1.call-start = ((), (), s32[]{:S(2)}) async-start(), calls=%async_computation.10 | async-start | bytes 12976128 | tf_op jit(solution)/shard_map/all_gather | solution.py:61
  58.9 242.3 %all-gather.16.cloned.1.call-start = ((), (), s32[]{:S(2)}) async-start(), calls=%async_computation.11 | async-start | bytes 6488064 | tf_op jit(solution)/shard_map/all_gather | solution.py:62
  59.5 271.7 %all-gather.12.cloned.1.call-start = ((), (), s32[]{:S(2)}) async-start(), calls=%async_computation.9 | async-start | bytes 2359296 | tf_op jit(solution)/shard_map/all_gather | solution.py:60
  60.1 425.4 %reduce-scatter.10.cloned.1.call-start = ((), (), s32[]{:S(2)}) async-start(), calls=%async_computation.12 | async-start | bytes 10485760 | tf_op jit(solution)/shard_map/reduce_scatter | solution.py:120
  70.7 126.9 %copy-start.15 = (f32[1024,16]{0,1:T(8,128)}, f32[1024,16]{0,1:T(8,128)S(1)}, u32[]{:S(2)}) copy-start(f32[1024,16]{0,1:T(8,128)S(1)} %get-tuple-element.419) | copy-start | bytes 196612
  70.7 126.9 %copy-start.17 = (f32[1024,16]{0,1:T(8,128)}, f32[1024,16]{0,1:T(8,128)S(1)}, u32[]{:S(2)}) copy-start(f32[1024,16]{0,1:T(8,128)S(1)} %get-tuple-element.418) | copy-start | bytes 196612
  232.4 98.7 %copy-start.11 = (bf16[64,8,2,512]{3,1,2,0:T(8,128)(2,1)}, bf16[64,8,2,512]{3,1,2,0:T(8,128)(2,1)S(1)}, u32[]{:S(2)}) copy-start(bf16[64,8,2,512]{3,1,2,0:T(8,128)(2,1)S(1)} %copy.82) | copy-start | bytes 3145732
  340.9 144.7 %copy-start.4 = (bf16[256,2048]{1,0:T(8,128)(2,1)S(1)}, bf16[256,2048]{1,0:T(8,128)(2,1)}, u32[]{:S(2)}) copy-start(bf16[256,2048]{1,0:T(8,128)(2,1)} %param.15) | copy-start | bytes 3145732
  340.9 144.7 %copy-start.9 = (bf16[256,2048]{1,0:T(8,128)(2,1)S(1)}, bf16[256,2048]{1,0:T(8,128)(2,1)}, u32[]{:S(2)}) copy-start(bf16[256,2048]{1,0:T(8,128)(2,1)} %param.16) | copy-start | bytes 3145732
  340.9 230.0 %all-gather.18.cloned.1.call-start = ((), (), s32[]{:S(2)}) async-start(), calls=%async_computation.13 | async-start | bytes 5242880 | tf_op jit(solution)/shard_map/all_gather | solution.py:134
  341.7 147.4 %copy-start.27 = (f32[256]{0:T(256)}, f32[256]{0:T(256)S(1)}, u32[]{:S(2)}) copy-start(f32[256]{0:T(256)S(1)} %compare_convert_fusion) | copy-start | bytes 3076
  489.2 338.4 %reduce-scatter.22.cloned.1.call-start = ((), (), s32[]{:S(2)}) async-start(), calls=%async_computation.19 | async-start | bytes 294912
  622.3 21.7 %copy-start.2 = (f32[1024,8,64]{0,2,1:T(8,128)}, f32[1024,8,64]{0,2,1:T(8,128)S(1)}, u32[]{:S(2)}) copy-start(f32[1024,8,64]{0,2,1:T(8,128)S(1)} %bitcast_add_fusion.5) | copy-start | bytes 6291460 | tf_op jit(solution)/shard_map/while
  622.3 21.7 %copy-start.20 = (f32[2,8,512,1]{2,1,3,0:T(8,128)S(1)}, f32[2,8,512,1]{2,1,3,0:T(8,128)}, u32[]{:S(2)}) copy-start(f32[2,8,512,1]{2,1,3,0:T(8,128)} %copy-done.19) | copy-start | bytes 98308 | tf_op jit(solution)/shard_map/while
  689.5 21.7 %copy-start.2 = (f32[1024,8,64]{0,2,1:T(8,128)}, f32[1024,8,64]{0,2,1:T(8,128)S(1)}, u32[]{:S(2)}) copy-start(f32[1024,8,64]{0,2,1:T(8,128)S(1)} %bitcast_add_fusion.5) | copy-start | bytes 6291460 | tf_op jit(solution)/shard_map/while
  689.5 21.7 %copy-start.20 = (f32[2,8,512,1]{2,1,3,0:T(8,128)S(1)}, f32[2,8,512,1]{2,1,3,0:T(8,128)}, u32[]{:S(2)}) copy-start(f32[2,8,512,1]{2,1,3,0:T(8,128)} %copy-done.19) | copy-start | bytes 98308 | tf_op jit(solution)/shard_map/while
  726.8 189.6 %reduce-scatter.12.cloned.1.call-start = ((), (), s32[]{:S(2)}) async-start(), calls=%async_computation.14 | async-start | bytes 10485760 | tf_op jit(solution)/shard_map/reduce_scatter | solution.py:197
  773.3 240.6 %reduce-scatter.14.cloned.1.call-start = ((), (), s32[]{:S(2)}) async-start(), calls=%async_computation.15 | async-start | bytes 14155776 | tf_op jit(solution)/shard_map/reduce_scatter | solution.py:218
  785.6 378.3 %reduce-scatter.18.cloned.1.call-start = ((), (), s32[]{:S(2)}) async-start(), calls=%async_computation.17 | async-start | bytes 25952256 | tf_op jit(solution)/shard_map/reduce_scatter | solution.py:221
  806.6 412.8 %reduce-scatter.16.cloned.1.call-start = ((), (), s32[]{:S(2)}) async-start(), calls=%async_computation.16 | async-start | bytes 4718592 | tf_op jit(solution)/shard_map/reduce_scatter | solution.py:220
  814.3 496.0 %reduce-scatter.20.cloned.1.call-start = ((), (), s32[]{:S(2)}) async-start(), calls=%async_computation.18 | async-start | bytes 12976128 | tf_op jit(solution)/shard_map/reduce_scatter | solution.py:222
  826.9 89.5 %copy-start.5 = (bf16[256,2048]{1,0:T(8,128)(2,1)S(1)}, bf16[256,2048]{1,0:T(8,128)(2,1)}, u32[]{:S(2)}) copy-start(bf16[256,2048]{1,0:T(8,128)(2,1)} %param.15) | copy-start | bytes 3145732
  826.9 89.5 %copy-start.7 = (f32[256,2048]{1,0:T(8,128)S(1)}, f32[256,2048]{1,0:T(8,128)}, u32[]{:S(2)}) copy-start(f32[256,2048]{1,0:T(8,128)} %reduce-scatter.10.cloned.1.call-done) | copy-start | bytes 6291460
  826.9 89.5 %copy-start.22 = (f32[2048]{0:T(1024)S(1)}, f32[2048]{0:T(1024)}, u32[]{:S(2)}) copy-start(f32[2048]{0:T(1024)} %copy-done.21) | copy-start | bytes 24580
  826.9 89.5 %copy-start.24 = (f32[256]{0:T(256)S(1)}, f32[256]{0:T(256)}, u32[]{:S(2)}) copy-start(f32[256]{0:T(256)} %copy-done.23) | copy-start | bytes 3076
  826.9 89.5 %copy-start.26 = (f32[256]{0:T(256)S(1)}, f32[256]{0:T(256)}, u32[]{:S(2)}) copy-start(f32[256]{0:T(256)} %copy-done.25) | copy-start | bytes 3076
  826.9 89.5 %copy-start.28 = (f32[256]{0:T(256)S(1)}, f32[256]{0:T(256)}, u32[]{:S(2)}) copy-start(f32[256]{0:T(256)} %copy-done.27) | copy-start | bytes 3076
  (18 other events, 84.1 us)
Sparse Core Ops, SparseCore 0:
  57.0 80.7 all-gather.7
  140.2 45.1 all-gather.9
  187.4 67.6 all-gather.13
  256.8 44.3 all-gather.15
  302.9 28.1 all-gather.11
  341.0 144.4 reduce-scatter.9
  489.3 81.4 all-gather.17
  726.9 32.1 reduce-scatter.21
  773.4 142.9 reduce-scatter.11
  920.1 93.7 reduce-scatter.13
  1018.0 145.9 reduce-scatter.17
  1168.1 51.2 reduce-scatter.15
  1223.5 86.7 reduce-scatter.19
where the time goes:
time: 1320 us
  waiting for transfers between devices  826 us (63%)
  matrix products  231 us (18%)
  blocking collectives  93.9 us (7%)
  local copies, waits for them, and re-layouts  81.9 us (6%)
  other arithmetic  59 us (4%)
  between operations  17.9 us (1%)
    reduce_scatter x1, waiting for transfers between devices, per_device(): lax.psum_scatter(grad_gu_w, 'fsdp', scatter_dimension=1, tiled=True)  147 us
    reduce_scatter x1, waiting for transfers between devices, per_device(): lax.psum_scatter(jnp.dot(attn_rows, w_out, preferred_element_type=jnp.flo...  144 us
    reduce_scatter x1, waiting for transfers between devices, per_device(): lax.psum_scatter(grad_down, 'fsdp', scatter_dimension=1, tiled=True)  90.9 us
    reduce_scatter x1, waiting for transfers between devices, per_device(): lax.psum_scatter(jnp.einsum('jse,jde->sd', grad_qkv, w_qkv, preferred_ele...  87.1 us
    all_gather x1, waiting for transfers between devices, per_device(): lax.all_gather(seed_rows.astype(jnp.bfloat16), 'tp', axis=0, tiled=True)  81.6 us
    all_gather x1, waiting for transfers between devices, per_device(): all_normed = lax.all_gather(normed, 'tp', axis=0, tiled=True)  67.1 us
    reduce_scatter x1, waiting for transfers between devices, per_device(): lax.psum_scatter(grad_out_w, 'fsdp', scatter_dimension=1, tiled=True)  52.1 us
    all_gather x1, waiting for transfers between devices, per_device(): lax.all_gather(qkv_weight, 'fsdp', axis=1, tiled=True)  47.7 us
  transfers between devices with their start and end apart: 13, of which 12 were waited for; matrix products, arithmetic and copies ran while one was open for 15% of the time, Pallas kernels for 0%

commit v1 on v0

--- a/solution.py
+++ b/solution.py
@@ -128,7 +128,7 @@
     mismatch = result - teacher.astype(jnp.float32)
     loss_part = jnp.sum(valid_rows[:, None] * mismatch * mismatch)
     count_part = jnp.sum(valid_rows)
-    loss_total, valid_total = lax.psum((loss_part, count_part), ("fsdp", "tp"))
+    loss_total, valid_total = lax.psum(lax.psum((loss_part, count_part), "fsdp"), "tp")
     loss_value = loss_total / (valid_total * D)
     seed_rows = valid_rows[:, None] * (out_grad.astype(jnp.float32) + mismatch)
     all_seed = lax.all_gather(seed_rows.astype(jnp.bfloat16), "tp", axis=0, tiled=True)

time: 1320 us -> 1330 us (level)
  blocking collectives: 93.9 us -> 117 us
  waiting for transfers between devices: 826 us -> 804 us
    unnamed x1 -> x2, blocking collectives: 42 us -> 80.1 us
    reduce_scatter x1, waiting for transfers between devices: 44.2 us -> 21.9 us  [per_device(): lax.psum_scatter(grad_qkv_w, 'fsdp', scatter_dimension=1, tiled=True)]
    psum x1 -> x2, blocking collectives: 41.6 us -> 26.3 us  [the longest x1 14.1 us: per_device(): lax.psum((loss_part, count_part), 'fsdp')]
where the time goes in v1:
time: 1330 us; the launch traced here: 1320 us
  waiting for transfers between devices  804 us (60%)
  matrix products  231 us (17%)
  blocking collectives  117 us (9%)
  local copies, waits for them, and re-layouts  81.9 us (6%)
  other arithmetic  59.1 us (4%)
  between operations  17.9 us (1%)
    reduce_scatter x1, waiting for transfers between devices, per_device(): lax.psum_scatter(grad_gu_w, 'fsdp', scatter_dimension=1, tiled=True)  147 us
    reduce_scatter x1, waiting for transfers between devices, per_device(): lax.psum_scatter(jnp.dot(attn_rows, w_out, preferred_element_type=jnp.flo...  144 us
    reduce_scatter x1, waiting for transfers between devices, per_device(): lax.psum_scatter(grad_down, 'fsdp', scatter_dimension=1, tiled=True)  90.9 us
    reduce_scatter x1, waiting for transfers between devices, per_device(): lax.psum_scatter(jnp.einsum('jse,jde->sd', grad_qkv, w_qkv, preferred_ele...  87.1 us
    all_gather x1, waiting for transfers between devices, per_device(): lax.all_gather(seed_rows.astype(jnp.bfloat16), 'tp', axis=0, tiled=True)  81.6 us
    unnamed x2, blocking collectives  80.1 us
    all_gather x1, waiting for transfers between devices, per_device(): all_normed = lax.all_gather(normed, 'tp', axis=0, tiled=True)  67.1 us
    reduce_scatter x1, waiting for transfers between devices, per_device(): lax.psum_scatter(grad_out_w, 'fsdp', scatter_dimension=1, tiled=True)  52.1 us
  transfers between devices with their start and end apart: 13, of which 12 were waited for; matrix products, arithmetic and copies ran while one was open for 15% of the time, Pallas kernels for 0%

profile of v1, /device:TPU:0, one launch (start us, length us, event | category | flops | bytes accessed | tf_op | source)
XLA Modules:
  0.0 1318.6 jit_solution(9600857503685326756)
XLA Ops:
  12.2 42.0 %all-reduce.5 = (f32[2048]{0:T(1024)S(1)}, f32[2048]{0:T(1024)S(1)}) all-reduce(f32[2048]{0:T(1024)S(1)} %dynamic-update-slice.1, f32[2048]{0:T(1024)S(1)} %dynamic-update-slice), channel_id=1, replica_groups=mesh['fsdp'=8,'tp'=4] {'fsdp','tp'}, use_global_device_ids=true, to_apply=%add.1 | all-reduce | flops 4096 | bytes 32768
  60.2 10.2 all-gather
  70.7 67.1 %all-gather.8.cloned.1.call-done = bf16[1024,2048]{1,0:T(8,128)(2,1)} async-done(((bf16[256,2048]{1,0:T(8,128)(2,1)}), bf16[1024,2048]{1,0:T(8,128)(2,1)}) %all-gather.8.cloned.1.call-update) | async-done | bytes 4194320 | tf_op jit(solution)/shard_map/all_gather | solution.py:73
  137.8 47.7 %all-gather.10.cloned.1.call-done = bf16[3,2048,512]{1,2,0:T(8,128)(2,1)} async-done(((bf16[3,256,512]{1,2,0:T(8,128)(2,1)}), bf16[3,2048,512]{1,2,0:T(8,128)(2,1)}) %all-gather.10.cloned.1.call-update) | async-done | bytes 6291472 | tf_op jit(solution)/shard_map/all_gather | solution.py:58
  185.5 10.1 add_bitcast_fusion
  199.0 32.1 %while.32 = (s32[]{:T(128)}, bf16[2,512,8,64]{1,3,2,0:T(8,128)(2,1)S(1)}, f32[2,8,512,1]{2,1,3,0:T(8,128)S(1)}, s32[2]{0:T(128)S(1)}, bf16[1024,8,64]{0,2,1:T(8,...) while((s32[]{:T(128)}, ...), condition=%wide.region_5.6_spmd.clone, body=%wide.region_2.5_spmd.clone.sunk | while | flops 1124594176 | bytes 56234364 | solution.py:115
  232.5 22.6 %all-gather.14.cloned.1.call-done = bf16[2,2048,1408]{2,1,0:T(8,128)(2,1)} async-done(((bf16[2,256,1408]{2,1,0:T(8,128)(2,1)}), bf16[2,2048,1408]{2,1,0:T(8,128)(2,1)}) %all-gather.14.cloned.1.call-update) | async-done | bytes 11534352 | tf_op jit(solution)/shard_map/all_gather | solution.py:61
  255.1 17.2 %convolution_bitcast_fusion.1 = f32[2,1024,1408]{2,1,0:T(8,128)S(1)} fusion(bf16[2,2048,1408]{2,1,0:T(8,128)(2,1)} %all-gather.14.cloned.1.call-done, bf16[1024,2048]{1,0:T(8,128)(2,1)} %all-gather.8.cloned.1.call-done), kind=kOutput, calls=%fused_computation.41 | convolution fusion | flops 11811160064 | bytes 27262976 | tf_op jit(solution)/shard_map/sd,jdf->jsf/dot_general | solution.py:117
  279.3 21.9 %all-gather.16.cloned.1.call-done = bf16[1408,2048]{1,0:T(8,128)(2,1)} async-done(((bf16[1408,256]{1,0:T(8,128)(2,1)}), bf16[1408,2048]{1,0:T(8,128)(2,1)}) %all-gather.16.cloned.1.call-update) | async-done | bytes 5767184 | tf_op jit(solution)/shard_map/all_gather | solution.py:62
  301.2 11.6 fusion.74
  312.9 18.3 %all-gather.12.cloned.1.call-done = bf16[512,2048]{1,0:T(8,128)(2,1)} async-done(((bf16[512,256]{1,0:T(8,128)(2,1)}), bf16[512,2048]{1,0:T(8,128)(2,1)}) %all-gather.12.cloned.1.call-update) | async-done | bytes 2097168 | tf_op jit(solution)/shard_map/all_gather | solution.py:60
  341.7 143.8 %reduce-scatter.10.cloned.1.call-done = f32[256,2048]{1,0:T(8,128)} async-done(((f32[1024,2048]{1,0:T(8,128)}), f32[256,2048]{1,0:T(8,128)}) %reduce-scatter.10.cloned.1.call-update) | async-done | bytes 2097168 | tf_op jit(solution)/shard_map/reduce_scatter | solution.py:120
  489.3 81.6 %all-gather.18.cloned.1.call-done = bf16[1024,2048]{1,0:T(8,128)(2,1)} async-done(((bf16[256,2048]{1,0:T(8,128)(2,1)}), bf16[1024,2048]{1,0:T(8,128)(2,1)}) %all-gather.18.cloned.1.call-update) | async-done | bytes 4194320 | tf_op jit(solution)/shard_map/all_gather | solution.py:134
  577.0 134.2 %while.33 = (s32[]{:T(128)}, f32[1024,8,64]{0,2,1:T(8,128)}, f32[1024,8,64]{0,2,1:T(8,128)}, f32[2,512,8,64]{1,0,3,2:T(2,128)}, s32[2]{0:T(128)S(1)}, /*index=5*...) while((s32[]{:T(128)}, f32[1024,8,64]{0,2,1:T(8,128)}, ...), condition=%wide.region_15.16_spmd.clone, body=%wide.region_13.15_spmd.clone.sunk | while | flops 2729701888 | bytes 200626816 | solution.py:180
  586.2 12.2 multiply_reduce_fusion.3
  624.3 19.7 %dynamic_update_slice.30 = f32[2,512,8,64]{1,0,3,2:T(2,128)} dynamic-update-slice(f32[2,512,8,64]{1,0,3,2:T(2,128)} %get-tuple-element.599, f32[1,512,8,64]{1,0,3,2:T(1,128)} %copy.85, s32[]{:T(128)S(6)} %copy.104, s32[]{:T(128)} %constant.200.clone.1..sunk.1, s32[]{:T(128)} %constant.200.clone.1..sunk.1, s32[]{:T(128)} %constant.200.clone.1..sunk.1) | dynamic-update-slice | bytes 2097156 | tf_op jit(solution)/shard_map/while/body/jit(dynamic_update_index_in_dim)/dynamic_update_slice | solution.py:115
  652.7 12.2 multiply_reduce_fusion.3
  691.4 19.7 %dynamic_update_slice.30 = f32[2,512,8,64]{1,0,3,2:T(2,128)} dynamic-update-slice(f32[2,512,8,64]{1,0,3,2:T(2,128)} %get-tuple-element.599, f32[1,512,8,64]{1,0,3,2:T(1,128)} %copy.85, s32[]{:T(128)S(6)} %copy.104, s32[]{:T(128)} %constant.200.clone.1..sunk.1, s32[]{:T(128)} %constant.200.clone.1..sunk.1, s32[]{:T(128)} %constant.200.clone.1..sunk.1) | dynamic-update-slice | bytes 2097156 | tf_op jit(solution)/shard_map/while/body/jit(dynamic_update_index_in_dim)/dynamic_update_slice | solution.py:115
  726.7 15.7 %fusion.34 = (bf16[1,1024,1408]{2,1,0:T(8,128)(2,1)}, bf16[1,1024,1408]{2,1,0:T(8,128)(2,1)}) fusion(f32[2,1024,1408]{2,1,0:T(8,128)} %copy-done.8, bf16[1024,2048]{1,0:T(8,128)(2,1)} %all-gather.18.cloned.1.call-done, bf16[1408,2048]{1,0:T(8,128)(2,1)} %all-gather.16.cloned.1.call-done), kind=kOutput, calls=%fused_computation.64 | convolution fusion | flops 5924323328 | bytes 27262976 | tf_op jit(solution)/shard_map/sd,fd->sf/dot_general | solution.py:148
  742.4 10.8 fusion.69
  753.2 20.0 %bitcast_add_fusion.2 = f32[1024,2048]{1,0:T(8,128)} fusion(f32[1024,2048,1]{1,0,2:T(8,128)} %fusion.69, bf16[2,2048,1408]{2,1,0:T(8,128)(2,1)} %all-gather.14.cloned.1.call-done, bf16[1,1024,1408]{2,1,0:T(8,128)(2,1)} %get-tuple-element.401, bf16[1,1024,1408]{2,1,0:T(8,128)(2,1)} %get-tuple-element.400), kind=kOutput, calls=%fused_computation.40 | convolution fusion | flops 11816140800 | bytes 34078720 | tf_op jit(solution)/shard_map/jsf,jdf->sd/dot_general | solution.py:199
  773.3 12.2 convolution_bitcast_fusion.2
  787.3 19.1 %convolution_bitcast_fusion = f32[2,2048,1408]{1,2,0:T(8,128)} fusion(bf16[1024,2048]{1,0:T(8,128)(2,1)} %all-gather.8.cloned.1.call-done, bf16[1,1024,1408]{2,1,0:T(8,128)(2,1)} %get-tuple-element.401, bf16[1,1024,1408]{2,1,0:T(8,128)(2,1)S(1)} %copy-done.30), kind=kOutput, calls=%fused_computation.39 | convolution fusion | flops 11814043648 | bytes 33030144 | tf_op jit(solution)/shard_map/sd,jsf->jdf/dot_general | solution.py:152
  816.1 10.8 fusion.76
  829.2 87.1 %reduce-scatter.12.cloned.1.call-done = f32[256,2048]{1,0:T(8,128)} async-done(((f32[1024,2048]{1,0:T(8,128)}), f32[256,2048]{1,0:T(8,128)}) %reduce-scatter.12.cloned.1.call-update) | async-done | bytes 2097168 | tf_op jit(solution)/shard_map/reduce_scatter | solution.py:197
  920.5 14.1 %all-reduce.6 = (f32[]{:T(128)}, f32[]{:T(128)}) all-reduce(f32[]{:T(128)} %get-tuple-element.353, f32[]{:T(128)} %fusion.68), channel_id=1, replica_groups=mesh['fsdp'=8,'tp'=4] {'fsdp'}, use_global_device_ids=true, to_apply=%region_8.9 | all-reduce | flops 2 | bytes 16 | tf_op jit(solution)/shard_map/psum | solution.py:131
  934.6 12.2 all-reduce.7
  946.8 38.0 %all-reduce.4 = (f32[2048]{0:T(1024)S(1)}, f32[2048]{0:T(1024)S(1)}) all-reduce(f32[2048]{0:T(1024)S(1)} %get-tuple-element.349, f32[2048]{0:T(1024)S(1)} %get-tuple-element.352), channel_id=4, replica_groups=mesh['fsdp'=8,'tp'=4] {'fsdp','tp'}, use_global_device_ids=true, to_apply=%region_20.21.clone | all-reduce | flops 4096 | bytes 32768
  992.4 21.9 %reduce-scatter.14.cloned.1.call-done = f32[3,256,512]{1,2,0:T(8,128)} async-done(((f32[3,2048,512]{1,2,0:T(8,128)}), f32[3,256,512]{1,2,0:T(8,128)}) %reduce-scatter.14.cloned.1.call-update) | async-done | bytes 1572880 | tf_op jit(solution)/shard_map/reduce_scatter | solution.py:218
  1017.3 147.0 %reduce-scatter.18.cloned.1.call-done = f32[2,256,1408]{1,2,0:T(8,128)} async-done(((f32[2,2048,1408]{1,2,0:T(8,128)}), f32[2,256,1408]{1,2,0:T(8,128)}) %reduce-scatter.18.cloned.1.call-update) | async-done | bytes 2883600 | tf_op jit(solution)/shard_map/reduce_scatter | solution.py:221
  1167.7 52.1 %reduce-scatter.16.cloned.1.call-done = f32[512,256]{1,0:T(8,128)} async-done(((f32[512,2048]{1,0:T(8,128)}), f32[512,256]{1,0:T(8,128)}) %reduce-scatter.16.cloned.1.call-update) | async-done | bytes 524304 | tf_op jit(solution)/shard_map/reduce_scatter | solution.py:220
  1219.8 90.9 %reduce-scatter.20.cloned.1.call-done = f32[1408,256]{1,0:T(8,128)} async-done(((f32[1408,2048]{1,0:T(8,128)}), f32[1408,256]{1,0:T(8,128)}) %reduce-scatter.20.cloned.1.call-update) | async-done | bytes 1441808 | tf_op jit(solution)/shard_map/reduce_scatter | solution.py:222
  (199 shorter events, 183.5 us)
Async XLA Ops:
  7.2 49.8 %copy-start.14 = (bf16[3,256,512]{2,1,0:T(8,128)(2,1)S(1)}, bf16[3,256,512]{2,1,0:T(8,128)(2,1)}, u32[]{:S(2)}) copy-start(bf16[3,256,512]{2,1,0:T(8,128)(2,1)} %param.21) | copy-start | bytes 2359300
  7.2 130.6 %all-gather.8.cloned.1.call-start = ((), (), s32[]{:S(2)}) async-start(), calls=%async_computation.7 | async-start | bytes 5242880 | tf_op jit(solution)/shard_map/all_gather | solution.py:73
  8.8 49.4 %copy-start.23 = (f32[256]{0:T(256)}, f32[256]{0:T(256)S(1)}, u32[]{:S(2)}) copy-start(f32[256]{0:T(256)S(1)} %broadcast_multiply_fusion.3) | copy-start | bytes 3076
  10.4 48.5 %copy-start.25 = (f32[256]{0:T(256)}, f32[256]{0:T(256)S(1)}, u32[]{:S(2)}) copy-start(f32[256]{0:T(256)S(1)} %add_rsqrt_fusion) | copy-start | bytes 3076
  56.9 128.6 %all-gather.10.cloned.1.call-start = ((), (), s32[]{:S(2)}) async-start(), calls=%async_computation.8 | async-start | bytes 7077888 | tf_op jit(solution)/shard_map/all_gather | solution.py:58
  58.2 196.9 %all-gather.14.cloned.1.call-start = ((), (), s32[]{:S(2)}) async-start(), calls=%async_computation.10 | async-start | bytes 12976128 | tf_op jit(solution)/shard_map/all_gather | solution.py:61
  58.9 242.3 %all-gather.16.cloned.1.call-start = ((), (), s32[]{:S(2)}) async-start(), calls=%async_computation.11 | async-start | bytes 6488064 | tf_op jit(solution)/shard_map/all_gather | solution.py:62
  59.5 271.7 %all-gather.12.cloned.1.call-start = ((), (), s32[]{:S(2)}) async-start(), calls=%async_computation.9 | async-start | bytes 2359296 | tf_op jit(solution)/shard_map/all_gather | solution.py:60
  60.1 425.4 %reduce-scatter.10.cloned.1.call-start = ((), (), s32[]{:S(2)}) async-start(), calls=%async_computation.12 | async-start | bytes 10485760 | tf_op jit(solution)/shard_map/reduce_scatter | solution.py:120
  70.7 126.9 %copy-start.15 = (f32[1024,16]{0,1:T(8,128)}, f32[1024,16]{0,1:T(8,128)S(1)}, u32[]{:S(2)}) copy-start(f32[1024,16]{0,1:T(8,128)S(1)} %get-tuple-element.421) | copy-start | bytes 196612
  70.7 126.9 %copy-start.17 = (f32[1024,16]{0,1:T(8,128)}, f32[1024,16]{0,1:T(8,128)S(1)}, u32[]{:S(2)}) copy-start(f32[1024,16]{0,1:T(8,128)S(1)} %get-tuple-element.420) | copy-start | bytes 196612
  232.5 98.7 %copy-start.11 = (bf16[64,8,2,512]{3,1,2,0:T(8,128)(2,1)}, bf16[64,8,2,512]{3,1,2,0:T(8,128)(2,1)S(1)}, u32[]{:S(2)}) copy-start(bf16[64,8,2,512]{3,1,2,0:T(8,128)(2,1)S(1)} %copy.82) | copy-start | bytes 3145732
  340.8 144.7 %copy-start.4 = (bf16[256,2048]{1,0:T(8,128)(2,1)S(1)}, bf16[256,2048]{1,0:T(8,128)(2,1)}, u32[]{:S(2)}) copy-start(bf16[256,2048]{1,0:T(8,128)(2,1)} %param.15) | copy-start | bytes 3145732
  340.8 144.7 %copy-start.9 = (bf16[256,2048]{1,0:T(8,128)(2,1)S(1)}, bf16[256,2048]{1,0:T(8,128)(2,1)}, u32[]{:S(2)}) copy-start(bf16[256,2048]{1,0:T(8,128)(2,1)} %param.16) | copy-start | bytes 3145732
  340.9 230.0 %all-gather.18.cloned.1.call-start = ((), (), s32[]{:S(2)}) async-start(), calls=%async_computation.13 | async-start | bytes 5242880 | tf_op jit(solution)/shard_map/all_gather | solution.py:134
  341.7 147.4 %copy-start.27 = (f32[256]{0:T(256)}, f32[256]{0:T(256)S(1)}, u32[]{:S(2)}) copy-start(f32[256]{0:T(256)S(1)} %compare_convert_fusion) | copy-start | bytes 3076
  489.2 338.3 %reduce-scatter.22.cloned.1.call-start = ((), (), s32[]{:S(2)}) async-start(), calls=%async_computation.19 | async-start | bytes 294912
  622.2 21.7 %copy-start.2 = (f32[1024,8,64]{0,2,1:T(8,128)}, f32[1024,8,64]{0,2,1:T(8,128)S(1)}, u32[]{:S(2)}) copy-start(f32[1024,8,64]{0,2,1:T(8,128)S(1)} %bitcast_add_fusion.5) | copy-start | bytes 6291460 | tf_op jit(solution)/shard_map/while
  622.2 21.7 %copy-start.20 = (f32[2,8,512,1]{2,1,3,0:T(8,128)S(1)}, f32[2,8,512,1]{2,1,3,0:T(8,128)}, u32[]{:S(2)}) copy-start(f32[2,8,512,1]{2,1,3,0:T(8,128)} %copy-done.19) | copy-start | bytes 98308 | tf_op jit(solution)/shard_map/while
  689.3 21.7 %copy-start.2 = (f32[1024,8,64]{0,2,1:T(8,128)}, f32[1024,8,64]{0,2,1:T(8,128)S(1)}, u32[]{:S(2)}) copy-start(f32[1024,8,64]{0,2,1:T(8,128)S(1)} %bitcast_add_fusion.5) | copy-start | bytes 6291460 | tf_op jit(solution)/shard_map/while
  689.4 21.7 %copy-start.20 = (f32[2,8,512,1]{2,1,3,0:T(8,128)S(1)}, f32[2,8,512,1]{2,1,3,0:T(8,128)}, u32[]{:S(2)}) copy-start(f32[2,8,512,1]{2,1,3,0:T(8,128)} %copy-done.19) | copy-start | bytes 98308 | tf_op jit(solution)/shard_map/while
  726.6 189.7 %reduce-scatter.12.cloned.1.call-start = ((), (), s32[]{:S(2)}) async-start(), calls=%async_computation.14 | async-start | bytes 10485760 | tf_op jit(solution)/shard_map/reduce_scatter | solution.py:197
  773.2 241.1 %reduce-scatter.14.cloned.1.call-start = ((), (), s32[]{:S(2)}) async-start(), calls=%async_computation.15 | async-start | bytes 14155776 | tf_op jit(solution)/shard_map/reduce_scatter | solution.py:218
  785.5 378.8 %reduce-scatter.18.cloned.1.call-start = ((), (), s32[]{:S(2)}) async-start(), calls=%async_computation.17 | async-start | bytes 25952256 | tf_op jit(solution)/shard_map/reduce_scatter | solution.py:221
  806.5 413.3 %reduce-scatter.16.cloned.1.call-start = ((), (), s32[]{:S(2)}) async-start(), calls=%async_computation.16 | async-start | bytes 4718592 | tf_op jit(solution)/shard_map/reduce_scatter | solution.py:220
  814.3 496.4 %reduce-scatter.20.cloned.1.call-start = ((), (), s32[]{:S(2)}) async-start(), calls=%async_computation.18 | async-start | bytes 12976128 | tf_op jit(solution)/shard_map/reduce_scatter | solution.py:222
  826.8 89.5 %copy-start.5 = (bf16[256,2048]{1,0:T(8,128)(2,1)S(1)}, bf16[256,2048]{1,0:T(8,128)(2,1)}, u32[]{:S(2)}) copy-start(bf16[256,2048]{1,0:T(8,128)(2,1)} %param.15) | copy-start | bytes 3145732
  826.8 89.5 %copy-start.7 = (f32[256,2048]{1,0:T(8,128)S(1)}, f32[256,2048]{1,0:T(8,128)}, u32[]{:S(2)}) copy-start(f32[256,2048]{1,0:T(8,128)} %reduce-scatter.10.cloned.1.call-done) | copy-start | bytes 6291460
  826.8 89.5 %copy-start.22 = (f32[2048]{0:T(1024)S(1)}, f32[2048]{0:T(1024)}, u32[]{:S(2)}) copy-start(f32[2048]{0:T(1024)} %copy-done.21) | copy-start | bytes 24580
  826.8 89.5 %copy-start.24 = (f32[256]{0:T(256)S(1)}, f32[256]{0:T(256)}, u32[]{:S(2)}) copy-start(f32[256]{0:T(256)} %copy-done.23) | copy-start | bytes 3076
  826.8 89.5 %copy-start.26 = (f32[256]{0:T(256)S(1)}, f32[256]{0:T(256)}, u32[]{:S(2)}) copy-start(f32[256]{0:T(256)} %copy-done.25) | copy-start | bytes 3076
  826.8 89.5 %copy-start.28 = (f32[256]{0:T(256)S(1)}, f32[256]{0:T(256)}, u32[]{:S(2)}) copy-start(f32[256]{0:T(256)} %copy-done.27) | copy-start | bytes 3076
  (18 other events, 84.1 us)
Sparse Core Ops, SparseCore 0:
  57.0 80.7 all-gather.7
  140.2 45.1 all-gather.9
  187.4 67.6 all-gather.13
  256.8 44.3 all-gather.15
  302.9 28.1 all-gather.11
  341.0 144.4 reduce-scatter.9
  489.3 81.4 all-gather.17
  726.7 32.1 reduce-scatter.21
  773.3 142.9 reduce-scatter.11
  920.1 94.1 reduce-scatter.13
  1018.3 145.9 reduce-scatter.17
  1168.4 51.2 reduce-scatter.15
  1223.9 86.7 reduce-scatter.19
